TPU v7x, 32 devices: a whole 2x2x4 slice. The times are simulated.
32 devices in a mesh: parts: 2 (over y), vocab: 4 (over z), mp: 2 (over x), rep: 2 (over core).
Axes of the slice: x: 2, y: 2, z: 4, core: 2. Of those that a mesh axis runs over, the one named last changes fastest.
Arguments:
- resid_base: bfloat16 [128, 4608], P(('parts', 'vocab', 'rep'), 'mp'), parts along dimension 0, may hold values from -60 to 60
- mlp_hidden: bfloat16 [128, 36864], P(('parts', 'vocab', 'rep'), 'mp'), parts along dimension 0, may hold values from -6 to 6
- edit_in: float32 [73728], P(('parts', 'mp')), parts along dimension 0, may hold values from -0.03125 to 0.03125
- edit_out: float32 [9216], P(('parts', 'mp')), parts along dimension 0, may hold values from -6 to 6
- norm_gain: float32 [4608], P('mp'), may hold values from 0.5 to 1.5
- head: bfloat16 [4608, 8192], P(None, ('vocab', 'mp', 'rep')), may hold values from -0.25 to 0.25
- token_ids: int32 [128], P('parts'), parts along dimension 0, may hold values from 0 to 8191
Outputs:
- penalty: float32 [128], P(('parts', 'vocab', 'rep')), parts along dimension 0
- grad_in: float32 [73728], P(('parts', 'mp')), parts along dimension 0
- grad_out: float32 [9216], P(('parts', 'mp')), parts along dimension 0
There are 2 independent parts, one for each index of `parts`. A program takes and returns all parts, laid end to end along the dimension named above; an argument that names none is the same for every part. Nothing has to cross between parts.
All inputs are finite; a program needn't handle non-finite values.
Results may differ from a plain program's by a relative error of at most 0.011.
Values may be sent and summed in bfloat16 or wider, within the bound.
No kernel may reach another device: no remote copies, remote signals or barrier semaphores. Data moves between devices by JAX's collectives and lax.ppermute only.
A program may use at most 64 MiB of HBM per device.

v0:
```python
import jax
import jax.numpy as jnp
from jax import lax
from jax.sharding import PartitionSpec as P

D = 4608
softcap = 30.0
epsilon = 1e-06


def local(resid_base, mlp_hidden, edit_in, edit_out, norm_gain, head, token_ids):
    tok_rows = resid_base.shape[0]
    feat_cols = resid_base.shape[1]
    voc_cols = head.shape[1]
    hidden_f = mlp_hidden.astype(jnp.float32)
    base_f = resid_base.astype(jnp.float32)
    mix_part = jnp.sum(hidden_f * edit_in[None, :], axis=1)
    mix_scale, square_base, base_along, out_square = lax.psum(
        (
            mix_part,
            jnp.sum(base_f * base_f, axis=1),
            jnp.sum(base_f * edit_out[None, :], axis=1),
            jnp.sum(edit_out * edit_out),
        ),
        "mp",
    )
    resid = base_f + mix_scale[:, None] * edit_out[None, :]
    square_edit = square_base + 2.0 * mix_scale * base_along + mix_scale * mix_scale * out_square
    along = base_along + mix_scale * out_square
    edit_scale = lax.rsqrt(square_edit / D + epsilon)
    base_scale = lax.rsqrt(square_base / D + epsilon)
    x_edit = (resid * edit_scale[:, None] * norm_gain[None, :]).astype(jnp.bfloat16)
    x_base = (base_f * base_scale[:, None] * norm_gain[None, :]).astype(jnp.bfloat16)
    stacked = jnp.stack([x_edit, x_base], axis=0)
    direction = lax.all_gather(edit_out * norm_gain, "mp", axis=0, tiled=True)
    weights_all = lax.all_gather(mix_scale * edit_scale, ("vocab", "rep"), axis=0, tiled=True)
    full_cols = lax.all_gather(stacked, "mp", axis=2, tiled=True)
    logits_pre = jnp.einsum(
        "ktd,dv->ktv",
        lax.all_gather(full_cols, ("vocab", "rep"), axis=1, tiled=True),
        head,
        preferred_element_type=jnp.float32,
    )
    capped = softcap * jnp.tanh(logits_pre / softcap)
    totals = lax.psum(jnp.sum(jnp.exp(capped), axis=2), ("vocab", "mp", "rep"))
    log_totals = jnp.log(totals)
    probs = jnp.exp(capped - log_totals[:, :, None])
    z_edit = capped[0]
    z_base = capped[1]
    first_col = lax.axis_index(("vocab", "mp", "rep")) * voc_cols
    columns = first_col + jnp.arange(voc_cols, dtype=jnp.int32)
    onehot = (token_ids[:, None] == columns[None, :]).astype(jnp.float32)
    diff = z_base - z_edit
    kl_part = jnp.sum(probs[1] * diff, axis=1)
    gap_part = jnp.sum(onehot * diff, axis=1)
    dy_rows = ((2.0 * probs[0] - probs[1] - onehot) * (1.0 - (z_edit / softcap) ** 2)).astype(
        jnp.bfloat16
    )
    dx_part = lax.dot_general(
        dy_rows, head, (((1,), (1,)), ((), ())), preferred_element_type=jnp.float32
    )
    align_part = jnp.sum(logits_pre[0] * dy_rows.astype(jnp.float32), axis=1)
    proj_part = jnp.dot(dx_part, direction, precision=lax.Precision.HIGHEST)
    weighted_part = jnp.dot(weights_all, dx_part, precision=lax.Precision.HIGHEST)
    kl_all, gap_all, proj_all, align_all, weighted_all = lax.psum(
        (kl_part, gap_part, proj_part, align_part, weighted_part), ("vocab", "mp", "rep")
    )
    tok_start = lax.axis_index(("vocab", "rep")) * tok_rows
    feat_start = lax.axis_index("mp") * feat_cols
    kl_own = lax.dynamic_slice_in_dim(kl_all, tok_start, tok_rows, 0)
    gap_own = lax.dynamic_slice_in_dim(gap_all, tok_start, tok_rows, 0)
    proj_own = lax.dynamic_slice_in_dim(proj_all, tok_start, tok_rows, 0)
    align_own = lax.dynamic_slice_in_dim(align_all, tok_start, tok_rows, 0)
    lse_own = lax.dynamic_slice_in_dim(log_totals, tok_start, tok_rows, 1)
    penalty = kl_own + gap_own + 2.0 * (lse_own[0] - lse_own[1])
    normed = resid * edit_scale[:, None]
    shrink = edit_scale * align_own / D
    coeff = edit_scale * proj_own - shrink * (edit_scale * along)
    second_part = jnp.sum((mix_scale * shrink)[:, None] * normed, axis=0)
    grad_in_part = jnp.sum(coeff[:, None] * hidden_f, axis=0)
    second_sum, grad_in = lax.psum((second_part, grad_in_part), ("vocab", "rep"))
    weighted_own = lax.dynamic_slice_in_dim(weighted_all, feat_start, feat_cols, 0)
    grad_out = norm_gain * weighted_own - second_sum
    return (penalty, grad_in, grad_out)


def solution(mesh):
    in_specs = (
        P(("parts", "vocab", "rep"), "mp"),
        P(("parts", "vocab", "rep"), "mp"),
        P(("parts", "mp")),
        P(("parts", "mp")),
        P("mp"),
        P(None, ("vocab", "mp", "rep")),
        P("parts"),
    )
    out_specs = (P(("parts", "vocab", "rep")), P(("parts", "mp")), P(("parts", "mp")))
    return jax.shard_map(local, mesh=mesh, in_specs=in_specs, out_specs=out_specs, check_vma=False)
```

profile of v0, /device:TPU:8, one launch (start us, length us, event | category | flops | bytes accessed | tf_op | source)
XLA Modules:
  0.0 234.1 jit_solution(15880379331970252911)
XLA Ops:
  7.2 0.0 all-gather.3.cloned.1.call-start
  7.2 1.3 fusion.23
  8.6 0.9 fusion.15
  9.5 1.2 fusion.2
  10.7 1.2 dynamic-slice
  12.6 5.6 %all-reduce.2 = (f32[8]{0:T(128)S(1)}, f32[8]{0:T(128)S(1)}, f32[8]{0:T(128)S(1)}, f32[]{:T(128)}) all-reduce(f32[8]{0:T(128)S(1)} %get-tuple-element.6, f32[8]{0:T(128)S(1)} %fusion.2, f32[8]{0:T(128)S(1)} %get-tuple-element.5, f32[]{:T(128)} %get-tuple-element.26), channel_id=1, replica_groups=mesh['parts'=2,'vocab'=4,'mp'=2,'rep'=2] {'mp'}, use_global_device_ids=true, to_apply=%region_3.0 | all-reduce | flops 25 | bytes 200 | tf_op jit(solution)/shard_map/psum | solution.py:18
  18.2 0.7 multiply_dynamic-update-slice_fusion
  19.0 0.9 fusion.18
  19.9 5.1 %all_gather.12 = bf16[2,8,4608]{2,1,0:T(8,128)(2,1)} all-gather(bf16[2,8,2304]{2,1,0:T(8,128)(2,1)S(1)} %pad_maximum_fusion), channel_id=1, replica_groups=mesh['parts'=2,'vocab'=4,'mp'=2,'rep'=2] {'mp'}, dimensions={2}, use_global_device_ids=true | all-gather | bytes 221184 | tf_op jit(solution)/shard_map/all_gather | solution.py:37
  25.0 0.0 all-gather.3.cloned.1.call-update
  25.0 0.0 all-reduce.5.cloned.1.call-start
  25.1 10.7 %all-reduce = f32[64]{0:T(128)S(1)} all-reduce(f32[64]{0:T(128)S(1)} %get-tuple-element.15), channel_id=1, replica_groups=mesh['parts'=2,'vocab'=4,'mp'=2,'rep'=2] {'vocab','rep'}, use_global_device_ids=true, to_apply=%add | all-reduce | flops 64 | bytes 512
  35.8 4.4 %all-gather = f32[2,1,2304]{2,1,0:T(1,128)S(1)} all-gather(f32[1,1,2304]{2,1,0:T(1,128)S(1)} %reshape.34), channel_id=1, replica_groups=mesh['parts'=2,'vocab'=4,'mp'=2,'rep'=2] {'mp'}, dimensions={0}, use_global_device_ids=true | all-gather | bytes 27648 | tf_op jit(solution)/shard_map/all_gather | solution.py:35
  40.2 9.0 %all-gather.3.cloned.1.call-done = bf16[2,64,4608]{2,1,0:T(8,128)(2,1)} async-done(((bf16[2,8,4608]{2,1,0:T(8,128)(2,1)}), bf16[2,64,4608]{2,1,0:T(8,128)(2,1)}) %all-gather.3.cloned.1.call-update) | async-done | bytes 1179664 | tf_op jit(solution)/shard_map/all_gather | solution.py:40
  49.2 3.6 %exponential_reduce_fusion = (f32[2,64]{1,0:T(2,128)S(1)}, f32[2,64,512]{2,1,0:T(8,128)S(1)}) fusion(bf16[2,64,4608]{2,1,0:T(8,128)(2,1)} %all-gather.3.cloned.1.call-done, bf16[4608,512]{1,0:T(8,128)(2,1)} %param.12), kind=kOutput, calls=%fused_computation.9 | convolution fusion | flops 604176256 | bytes 6160896 | tf_op jit(solution)/shard_map/ktd,dv->ktv/dot_general | solution.py:38
  52.8 24.3 %psum.88 = f32[2,64]{1,0:T(2,128)S(1)} all-reduce(f32[2,64]{1,0:T(2,128)S(1)} %get-tuple-element.30), channel_id=1, replica_groups=mesh['parts'=2,'vocab'=4,'mp'=2,'rep'=2] {'vocab','mp','rep'}, use_global_device_ids=true, to_apply=%region_9.0 | all-reduce | flops 128 | bytes 1024 | tf_op jit(solution)/shard_map/psum | solution.py:45
  77.1 0.1 subtract_exponential_fusion
  77.2 0.2 fusion.9
  77.4 3.9 %fusion.24 = f32[64,4608]{1,0:T(8,128)S(1)} fusion(bf16[64,512]{1,0:T(8,128)(2,1)S(1)} %get-tuple-element.18, bf16[4608,512]{1,0:T(8,128)(2,1)} %param.12), kind=kOutput, calls=%fused_computation.54 | convolution fusion | flops 301989888 | bytes 5963776 | tf_op jit(solution)/shard_map/dot_general | solution.py:59
  81.3 0.7 convolution_reduce_fusion
  82.0 1.0 convolution_bitcast_fusion
  83.1 0.1 constant_dynamic-slice_fusion
  83.1 57.7 %all-reduce.1 = (f32[64]{0:T(128)S(1)}, f32[64]{0:T(128)S(1)}, f32[64]{0:T(128)S(1)}, f32[4608]{0:T(1024)S(1)}) all-reduce(f32[64]{0:T(128)S(1)} %add.92, f32[64]{0:T(128)S(1)} %convolution_bitcast_fusion, f32[64]{0:T(128)S(1)} %get-tuple-element.17, ...), channel_id=1, replica_groups=mesh['parts'=2,'vocab'=4,'mp'=2,'rep'=2] {'vocab','mp','rep'}, use_global_device_ids=true, to_apply=%region_11.0 | all-reduce | flops 4800 | bytes 38400 | tf_op jit(solution)/shard_map/psum | solution.py:65
  140.8 0.7 fusion.21
  141.5 0.1 multiply_reduce_fusion.1
  141.6 30.3 %psum.95 = f32[2304]{0:T(1024)S(1)} all-reduce(f32[2304]{0:T(1024)S(1)} %multiply_reduce_fusion.1), channel_id=1, replica_groups=mesh['parts'=2,'vocab'=4,'mp'=2,'rep'=2] {'vocab','rep'}, use_global_device_ids=true, to_apply=%region_21.0 | all-reduce | flops 2304 | bytes 18432 | tf_op jit(solution)/shard_map/psum | solution.py:81
  171.9 1.0 fusion.3
  172.9 0.0 all-reduce.5.cloned.1.call-update
  173.0 0.7 multiply_subtract_fusion
  173.6 0.6 bitcast_add_fusion
  174.2 51.5 %all-reduce.5.cloned.1.call-done = f32[18432]{0:T(1024)} async-done(((f32[18432]{0:T(1024)}), f32[18432]{0:T(1024)}) %all-reduce.5.cloned.1.call-update) | async-done | bytes 73744 | tf_op jit(solution)/shard_map/psum | solution.py:81
  225.7 1.5 copy.12
  (16 shorter events, 0.1 us)
Async XLA Ops:
  7.2 42.0 %all-gather.3.cloned.1.call-start = ((), (), s32[]{:S(2)}) async-start(), calls=%async_computation | async-start | bytes 1327104 | tf_op jit(solution)/shard_map/all_gather | solution.py:40
  25.0 200.7 %all-reduce.5.cloned.1.call-start = ((), (), s32[]{:S(2)}) async-start(), calls=%async_computation.1 | async-start | bytes 147456 | tf_op jit(solution)/shard_map/psum | solution.py:81
  40.2 37.0 %copy-start.4 = (s32[64]{0:T(128)S(1)}, s32[64]{0:T(128)}, u32[]{:S(2)}) copy-start(s32[64]{0:T(128)} %param.13) | copy-start | bytes 772
  81.3 60.2 %copy-start.1 = (bf16[8,2304]{1,0:T(8,128)(2,1)S(1)}, bf16[8,2304]{1,0:T(8,128)(2,1)}, u32[]{:S(2)}) copy-start(bf16[8,2304]{1,0:T(8,128)(2,1)} %param.7) | copy-start | bytes 110596
  81.3 60.2 %copy-start.2 = (f32[2304]{0:T(1024)S(1)}, f32[2304]{0:T(1024)}, u32[]{:S(2)}) copy-start(f32[2304]{0:T(1024)} %param.10) | copy-start | bytes 27652
  81.3 90.6 %copy-start = (bf16[8,18432]{1,0:T(8,128)(2,1)S(1)}, bf16[8,18432]{1,0:T(8,128)(2,1)}, u32[]{:S(2)}) copy-start(bf16[8,18432]{1,0:T(8,128)(2,1)} %param.8) | copy-start | bytes 884740
  82.0 90.9 %copy-start.3 = (f32[2304]{0:T(1024)S(1)}, f32[2304]{0:T(1024)}, u32[]{:S(2)}) copy-start(f32[2304]{0:T(1024)} %param.11) | copy-start | bytes 27652
Sparse Core Ops, SparseCore 0:
  25.1 24.0 all-gather.2
  173.1 52.6 all-reduce.4
where the time goes:
time: 235 us; the launch traced here: 234 us
  blocking collectives  138 us (59%)
  waiting for transfers between devices  60.5 us (26%)
  between operations  14.8 us (6%)
  matrix products  9.18 us (4%)
  other arithmetic  8.58 us (4%)
  local copies, waits for them, and re-layouts  2.88 us (1%)
    psum x1, blocking collectives, local(): lax.psum((kl_part, gap_part, proj_part, align_part, weighted_part), ('voc...  57.7 us
    psum x1, waiting for transfers between devices, local(): lax.psum((second_part, grad_in_part), ('vocab', 'rep'))  51.5 us
    psum x1, blocking collectives, local(): lax.psum((second_part, grad_in_part), ('vocab', 'rep'))  30.3 us
    psum x1, blocking collectives, local(): totals = lax.psum(jnp.sum(jnp.exp(capped), axis=2), ('vocab', 'mp', 'rep'))  24.3 us
    unnamed x1, blocking collectives  10.7 us
    all_gather x1, waiting for transfers between devices, local(): lax.all_gather(full_cols, ('vocab', 'rep'), axis=1, tiled=True)  9 us
    psum x1, blocking collectives, local(): lax.psum((mix_part, jnp.sum(base_f * base_f, axis=1), jnp.sum(base_f * ed...  5.58 us
    all_gather x1, blocking collectives, local(): full_cols = lax.all_gather(stacked, 'mp', axis=2, tiled=True)  5.14 us
  transfers between devices with their start and end apart: 2, of which 2 were waited for; matrix products, arithmetic and copies ran while one was open for 1% of the time, Pallas kernels for 0%

commit v1 on v0

--- a/solution.py
+++ b/solution.py
@@ -42,7 +42,8 @@
         preferred_element_type=jnp.float32,
     )
     capped = softcap * jnp.tanh(logits_pre / softcap)
-    totals = lax.psum(jnp.sum(jnp.exp(capped), axis=2), ("vocab", "mp", "rep"))
+    one_axis = lax.psum(jnp.sum(jnp.exp(capped), axis=2), ("mp", "rep"))
+    totals = lax.psum(one_axis, "vocab")
     log_totals = jnp.log(totals)
     probs = jnp.exp(capped - log_totals[:, :, None])
     z_edit = capped[0]

time: 235 us -> 220 us (0.936)
  blocking collectives: 138 us -> 123 us
    psum x1 -> x2, blocking collectives: 24.3 us -> 15.6 us  [the longest x1 8.82 us: local(): totals = lax.psum(one_axis, 'vocab')]
    psum x1, blocking collectives: 57.7 us -> 51.4 us  [local(): lax.psum((kl_part, gap_part, proj_part, align_part, weighted_part), ('voc...]
where the time goes in v1:
time: 220 us; the launch traced here: 219 us
  blocking collectives  123 us (56%)
  waiting for transfers between devices  60.5 us (28%)
  between operations  14.8 us (7%)
  matrix products  9.19 us (4%)
  other arithmetic  8.58 us (4%)
  local copies, waits for them, and re-layouts  2.88 us (1%)
    psum x1, waiting for transfers between devices, local(): lax.psum((second_part, grad_in_part), ('vocab', 'rep'))  51.5 us
    psum x1, blocking collectives, local(): lax.psum((kl_part, gap_part, proj_part, align_part, weighted_part), ('voc...  51.4 us
    psum x1, blocking collectives, local(): lax.psum((second_part, grad_in_part), ('vocab', 'rep'))  30.3 us
    unnamed x1, blocking collectives  10.7 us
    all_gather x1, waiting for transfers between devices, local(): lax.all_gather(full_cols, ('vocab', 'rep'), axis=1, tiled=True)  9 us
    psum x1, blocking collectives, local(): totals = lax.psum(one_axis, 'vocab')  8.82 us
    psum x1, blocking collectives, local(): one_axis = lax.psum(jnp.sum(jnp.exp(capped), axis=2), ('mp', 'rep'))  6.81 us
    psum x1, blocking collectives, local(): lax.psum((mix_part, jnp.sum(base_f * base_f, axis=1), jnp.sum(base_f * ed...  5.58 us
  transfers between devices with their start and end apart: 2, of which 2 were waited for; matrix products, arithmetic and copies ran while one was open for 1% of the time, Pallas kernels for 0%

profile of v1, /device:TPU:8, one launch (start us, length us, event | category | flops | bytes accessed | tf_op | source)
XLA Modules:
  0.0 219.2 jit_solution(3868964841620531896)
XLA Ops:
  7.2 0.0 all-gather.3.cloned.1.call-start
  7.2 1.3 fusion.23
  8.6 0.9 fusion.15
  9.5 1.2 fusion.2
  10.7 1.2 dynamic-slice
  12.6 5.6 %all-reduce.2 = (f32[8]{0:T(128)S(1)}, f32[8]{0:T(128)S(1)}, f32[8]{0:T(128)S(1)}, f32[]{:T(128)}) all-reduce(f32[8]{0:T(128)S(1)} %get-tuple-element.6, f32[8]{0:T(128)S(1)} %fusion.2, f32[8]{0:T(128)S(1)} %get-tuple-element.5, f32[]{:T(128)} %get-tuple-element.26), channel_id=1, replica_groups=mesh['parts'=2,'vocab'=4,'mp'=2,'rep'=2] {'mp'}, use_global_device_ids=true, to_apply=%region_3.0 | all-reduce | flops 25 | bytes 200 | tf_op jit(solution)/shard_map/psum | solution.py:18
  18.2 0.7 multiply_dynamic-update-slice_fusion
  19.0 0.9 fusion.18
  19.9 5.1 %all_gather.12 = bf16[2,8,4608]{2,1,0:T(8,128)(2,1)} all-gather(bf16[2,8,2304]{2,1,0:T(8,128)(2,1)S(1)} %pad_maximum_fusion), channel_id=1, replica_groups=mesh['parts'=2,'vocab'=4,'mp'=2,'rep'=2] {'mp'}, dimensions={2}, use_global_device_ids=true | all-gather | bytes 221184 | tf_op jit(solution)/shard_map/all_gather | solution.py:37
  25.0 0.0 all-gather.3.cloned.1.call-update
  25.0 0.0 all-reduce.5.cloned.1.call-start
  25.1 10.7 %all-reduce = f32[64]{0:T(128)S(1)} all-reduce(f32[64]{0:T(128)S(1)} %get-tuple-element.15), channel_id=1, replica_groups=mesh['parts'=2,'vocab'=4,'mp'=2,'rep'=2] {'vocab','rep'}, use_global_device_ids=true, to_apply=%add | all-reduce | flops 64 | bytes 512
  35.8 4.4 %all-gather = f32[2,1,2304]{2,1,0:T(1,128)S(1)} all-gather(f32[1,1,2304]{2,1,0:T(1,128)S(1)} %reshape.34), channel_id=1, replica_groups=mesh['parts'=2,'vocab'=4,'mp'=2,'rep'=2] {'mp'}, dimensions={0}, use_global_device_ids=true | all-gather | bytes 27648 | tf_op jit(solution)/shard_map/all_gather | solution.py:35
  40.2 9.0 %all-gather.3.cloned.1.call-done = bf16[2,64,4608]{2,1,0:T(8,128)(2,1)} async-done(((bf16[2,8,4608]{2,1,0:T(8,128)(2,1)}), bf16[2,64,4608]{2,1,0:T(8,128)(2,1)}) %all-gather.3.cloned.1.call-update) | async-done | bytes 1179664 | tf_op jit(solution)/shard_map/all_gather | solution.py:40
  49.2 3.6 %exponential_reduce_fusion = (f32[2,64]{1,0:T(2,128)S(1)}, f32[2,64,512]{2,1,0:T(8,128)S(1)}) fusion(bf16[2,64,4608]{2,1,0:T(8,128)(2,1)} %all-gather.3.cloned.1.call-done, bf16[4608,512]{1,0:T(8,128)(2,1)} %param.12), kind=kOutput, calls=%fused_computation.9 | convolution fusion | flops 604176256 | bytes 6160896 | tf_op jit(solution)/shard_map/ktd,dv->ktv/dot_general | solution.py:38
  52.8 6.8 %psum.95 = f32[2,64]{1,0:T(2,128)S(1)} all-reduce(f32[2,64]{1,0:T(2,128)S(1)} %get-tuple-element.30), channel_id=1, replica_groups=mesh['parts'=2,'vocab'=4,'mp'=2,'rep'=2] {'mp','rep'}, use_global_device_ids=true, to_apply=%region_9.0 | all-reduce | flops 128 | bytes 1024 | tf_op jit(solution)/shard_map/psum | solution.py:45
  59.6 8.8 %psum.96 = f32[2,64]{1,0:T(2,128)S(1)} all-reduce(f32[2,64]{1,0:T(2,128)S(1)} %psum.95), channel_id=1, replica_groups=mesh['parts'=2,'vocab'=4,'mp'=2,'rep'=2] {'vocab'}, use_global_device_ids=true, to_apply=%region_10.0 | all-reduce | flops 128 | bytes 1024 | tf_op jit(solution)/shard_map/psum | solution.py:46
  68.4 0.1 subtract_exponential_fusion
  68.6 0.2 fusion.9
  68.8 3.9 %fusion.24 = f32[64,4608]{1,0:T(8,128)S(1)} fusion(bf16[64,512]{1,0:T(8,128)(2,1)S(1)} %get-tuple-element.18, bf16[4608,512]{1,0:T(8,128)(2,1)} %param.12), kind=kOutput, calls=%fused_computation.54 | convolution fusion | flops 301989888 | bytes 5963776 | tf_op jit(solution)/shard_map/dot_general | solution.py:60
  72.7 0.7 convolution_reduce_fusion
  73.4 1.0 convolution_bitcast_fusion
  74.4 0.1 constant_dynamic-slice_fusion
  74.5 51.4 %all-reduce.1 = (f32[64]{0:T(128)S(1)}, f32[64]{0:T(128)S(1)}, f32[64]{0:T(128)S(1)}, f32[4608]{0:T(1024)S(1)}) all-reduce(f32[64]{0:T(128)S(1)} %add.94, f32[64]{0:T(128)S(1)} %convolution_bitcast_fusion, f32[64]{0:T(128)S(1)} %get-tuple-element.17, ...), channel_id=1, replica_groups=mesh['parts'=2,'vocab'=4,'mp'=2,'rep'=2] {'vocab','mp','rep'}, use_global_device_ids=true, to_apply=%region_12.0 | all-reduce | flops 4800 | bytes 38400 | tf_op jit(solution)/shard_map/psum | solution.py:66
  125.9 0.7 fusion.21
  126.6 0.1 multiply_reduce_fusion.1
  126.7 30.3 %psum.103 = f32[2304]{0:T(1024)S(1)} all-reduce(f32[2304]{0:T(1024)S(1)} %multiply_reduce_fusion.1), channel_id=1, replica_groups=mesh['parts'=2,'vocab'=4,'mp'=2,'rep'=2] {'vocab','rep'}, use_global_device_ids=true, to_apply=%region_22.0 | all-reduce | flops 2304 | bytes 18432 | tf_op jit(solution)/shard_map/psum | solution.py:82
  157.1 1.0 fusion.3
  158.1 0.7 multiply_subtract_fusion
  158.8 0.6 bitcast_add_fusion
  159.3 51.5 %all-reduce.5.cloned.1.call-done = f32[18432]{0:T(1024)} async-done(((f32[18432]{0:T(1024)}), f32[18432]{0:T(1024)}) %all-reduce.5.cloned.1.call-update) | async-done | bytes 73744 | tf_op jit(solution)/shard_map/psum | solution.py:82
  210.8 1.5 copy.12
  (17 shorter events, 0.1 us)
Async XLA Ops:
  7.2 42.0 %all-gather.3.cloned.1.call-start = ((), (), s32[]{:S(2)}) async-start(), calls=%async_computation | async-start | bytes 1327104 | tf_op jit(solution)/shard_map/all_gather | solution.py:40
  25.0 185.8 %all-reduce.5.cloned.1.call-start = ((), (), s32[]{:S(2)}) async-start(), calls=%async_computation.1 | async-start | bytes 147456 | tf_op jit(solution)/shard_map/psum | solution.py:82
  40.2 28.4 %copy-start.4 = (s32[64]{0:T(128)S(1)}, s32[64]{0:T(128)}, u32[]{:S(2)}) copy-start(s32[64]{0:T(128)} %param.13) | copy-start | bytes 772
  72.7 54.0 %copy-start.1 = (bf16[8,2304]{1,0:T(8,128)(2,1)S(1)}, bf16[8,2304]{1,0:T(8,128)(2,1)}, u32[]{:S(2)}) copy-start(bf16[8,2304]{1,0:T(8,128)(2,1)} %param.7) | copy-start | bytes 110596
  72.7 53.9 %copy-start.2 = (f32[2304]{0:T(1024)S(1)}, f32[2304]{0:T(1024)}, u32[]{:S(2)}) copy-start(f32[2304]{0:T(1024)} %param.10) | copy-start | bytes 27652
  72.7 84.3 %copy-start = (bf16[8,18432]{1,0:T(8,128)(2,1)S(1)}, bf16[8,18432]{1,0:T(8,128)(2,1)}, u32[]{:S(2)}) copy-start(bf16[8,18432]{1,0:T(8,128)(2,1)} %param.8) | copy-start | bytes 884740
  73.4 84.7 %copy-start.3 = (f32[2304]{0:T(1024)S(1)}, f32[2304]{0:T(1024)}, u32[]{:S(2)}) copy-start(f32[2304]{0:T(1024)} %param.11) | copy-start | bytes 27652
Sparse Core Ops, SparseCore 0:
  25.1 24.0 all-gather.2
  158.2 52.5 all-reduce.4
